TPU v7x, 32 devices: a whole 2x2x4 slice. The times are simulated.
32 devices in a mesh: dp: 8 (over z, core), tensor: 4 (over y, x).
Axes of the slice: x: 2, y: 2, z: 4, core: 2. Of those that a mesh axis runs over, the one named last changes fastest.
Arguments:
- tokens: bfloat16 [8192, 2048], P('dp'), may hold values from -6 to 6
- lengths: int32 [64], P('dp'), may hold values from 1 to 64, 2560 in all
- cotangent: bfloat16 [8192, 2048], P('dp'), may hold values from -6 to 6
- pre_gain: float32 [2048], replicated, may hold values from 0.5 to 1.5
- pre_shift: float32 [2048], replicated, may hold values from -1.5 to 1.5
- qkv_weight: bfloat16 [3, 2048, 2048], P(None, None, 'tensor'), may hold values from -0.125 to 0.125
- qkv_bias: float32 [3, 2048], P(None, 'tensor'), may hold values from -1.5 to 1.5
- mix_gain: float32 [2048], P('tensor'), may hold values from 0.5 to 1.5
- mix_shift: float32 [2048], P('tensor'), may hold values from -1.5 to 1.5
- out_weight: bfloat16 [2048, 2048], P('tensor'), may hold values from -0.125 to 0.125
- out_bias: float32 [2048], replicated, may hold values from -1.5 to 1.5
- ffn_gain: float32 [2048], replicated, may hold values from 0.5 to 1.5
- ffn_shift: float32 [2048], replicated, may hold values from -1.5 to 1.5
- up_weight: bfloat16 [2048, 8192], P(None, 'tensor'), may hold values from -0.125 to 0.125
- up_bias: float32 [8192], P('tensor'), may hold values from -2.5 to 2.5
- hid_gain: float32 [8192], P('tensor'), may hold values from 0.5 to 1.5
- hid_shift: float32 [8192], P('tensor'), may hold values from -1.5 to 1.5
- down_weight: bfloat16 [8192, 2048], P('tensor'), may hold values from -0.0625 to 0.0625
- down_bias: float32 [2048], replicated, may hold values from -1.5 to 1.5
Outputs:
- output: bfloat16 [8192, 2048], P('dp')
- tokens_grad: float32 [8192, 2048], P('dp')
- pre_gain_grad: float32 [2048], replicated
- pre_shift_grad: float32 [2048], replicated
- qkv_weight_grad: float32 [3, 2048, 2048], P(None, 'dp', 'tensor')
- qkv_bias_grad: float32 [3, 2048], P(None, 'tensor')
- mix_gain_grad: float32 [2048], P('tensor')
- mix_shift_grad: float32 [2048], P('tensor')
- out_weight_grad: float32 [2048, 2048], P('tensor', 'dp')
- out_bias_grad: float32 [2048], replicated
- ffn_gain_grad: float32 [2048], replicated
- ffn_shift_grad: float32 [2048], replicated
- up_weight_grad: float32 [2048, 8192], P('dp', 'tensor')
- up_bias_grad: float32 [8192], P('tensor')
- hid_gain_grad: float32 [8192], P('tensor')
- hid_shift_grad: float32 [8192], P('tensor')
- down_weight_grad: float32 [8192, 2048], P('tensor', 'dp')
- down_bias_grad: float32 [2048], replicated
Inputs may be any that keep to these rules, and one draw needn't show every extreme that they name: Caption length of each pair; the lengths sum to 2560 and the longest is 64.
All inputs are finite; a program needn't handle non-finite values. No bound on the sum of `lengths` on one device may be relied on, other than what follows from the above.
Results may differ from a plain program's by a relative error of at most 0.013.
Values sent between devices are 32-bit elements; how exact they have to be, the bound alone decides.
No kernel may reach another device: no remote copies, remote signals or barrier semaphores. Data moves between devices by JAX's collectives and lax.ppermute only.
A program may use at most 256 MiB of HBM per device.

v0:
```python
import math
import jax
import jax.numpy as jnp
from jax import lax
from jax.sharding import PartitionSpec as P

D = 2048
HD = 64
FF = 8192
SLOT = 128
IMG = 64
SCALE_BASE = 512
eps = 1e-05
root_half = 0.7071067811865476
inv_root_two_pi = 0.3989422804014327
masked_score = -1e30


def rounded(value):
    return value.astype(jnp.bfloat16)


def tables():
    place = jnp.arange(SLOT, dtype=jnp.float32)
    index = jnp.arange(HD // 2, dtype=jnp.float32)
    theta = 10000.0 ** (-2.0 * index / HD)
    angle = place[:, None] * theta[None, :]
    zeta = (2.0 * index + 0.4 * HD) / (1.4 * HD)
    growth = zeta[None, :] ** ((place[:, None] - SLOT // 2) / SCALE_BASE)
    return (jnp.cos(angle), jnp.sin(angle), growth)


def rotate(value, cosine, sine, factor):
    shape = value.shape
    pairs = value.reshape(shape[:-1] + (shape[-1] // 2, 2))
    even = pairs[..., 0]
    odd = pairs[..., 1]
    cos_b = cosine[:, None, :]
    sin_b = sine[:, None, :]
    fac_b = factor[:, None, :]
    new_even = (even * cos_b - odd * sin_b) * fac_b
    new_odd = (odd * cos_b + even * sin_b) * fac_b
    return jnp.stack([new_even, new_odd], axis=-1).reshape(shape)


def local_norm(value):
    mean = jnp.mean(value, axis=-1, keepdims=True)
    var = jnp.mean(value * value, axis=-1, keepdims=True) - mean * mean
    inverse = lax.rsqrt(var + eps)
    return ((value - mean) * inverse, inverse)


def local_back(grad, hat, gain, inverse):
    scaled = grad * gain
    return inverse * (
        scaled
        - jnp.mean(scaled, axis=-1, keepdims=True)
        - hat * jnp.mean(scaled * hat, axis=-1, keepdims=True)
    )


def body(
    tokens,
    lengths,
    cotangent,
    pre_gain,
    pre_shift,
    qkv_weight,
    qkv_bias,
    mix_gain,
    mix_shift,
    out_weight,
    out_bias,
    ffn_gain,
    ffn_shift,
    up_weight,
    up_bias,
    hid_gain,
    hid_shift,
    down_weight,
    down_bias,
):
    pairs = lengths.shape[0]
    rows = tokens.shape[0]
    local_width = qkv_weight.shape[2]
    local_heads = local_width // HD
    scale = 1.0 / math.sqrt(HD)
    cosine, sine, growth = tables()
    shrink = 1.0 / growth
    place = jnp.arange(SLOT, dtype=jnp.int32)
    causal = (place[None, :] <= place[:, None])[None, None]
    valid = place[None, None, None, :] < (IMG + lengths)[:, None, None, None]
    allowed = causal & valid
    inputs = tokens.astype(jnp.float32)
    pre_hat, pre_inv = local_norm(inputs)
    first = rounded(pre_hat * pre_gain + pre_shift)
    proj = (
        jnp.einsum("td,cde->cte", first, qkv_weight, preferred_element_type=jnp.float32)
        + qkv_bias[:, None, :]
    )
    shaped = proj.reshape(3, pairs, SLOT, local_heads, HD)
    query = rounded(rotate(shaped[0], cosine, sine, growth))
    key = rounded(rotate(shaped[1], cosine, sine, shrink))
    value = rounded(shaped[2])

    def scores_of():
        raw = jnp.einsum("pqhd,pkhd->phqk", query, key, preferred_element_type=jnp.float32) * scale
        return jnp.where(allowed, raw, masked_score)

    scores = scores_of()
    top = jnp.max(scores, axis=-1, keepdims=True)
    expd = jnp.exp(scores - top)
    total = jnp.sum(expd, axis=-1, keepdims=True)
    probs = expd / total
    log_total = top + jnp.log(total)
    mixed = jnp.einsum(
        "phqk,pkhd->pqhd", rounded(probs), value, preferred_element_type=jnp.float32
    ).reshape(rows, local_width)
    mix_sums = lax.psum((jnp.sum(mixed, 1), jnp.sum(mixed * mixed, 1)), "tensor")
    mix_mean = mix_sums[0] / D
    mix_inv = lax.rsqrt(mix_sums[1] / D - mix_mean * mix_mean + eps)
    mix_hat = (mixed - mix_mean[:, None]) * mix_inv[:, None]
    mix_low = rounded(mix_hat * mix_gain + mix_shift)
    branch = lax.psum(jnp.dot(mix_low, out_weight, preferred_element_type=jnp.float32), "tensor")
    middle = inputs + branch + out_bias
    ffn_hat, ffn_inv = local_norm(middle)
    second = rounded(ffn_hat * ffn_gain + ffn_shift)
    hidden = jnp.dot(second, up_weight, preferred_element_type=jnp.float32) + up_bias
    active = jax.nn.gelu(hidden, approximate=False)
    hid_sums = lax.psum((jnp.sum(active, 1), jnp.sum(active * active, 1)), "tensor")
    hid_mean = hid_sums[0] / FF
    hid_inv = lax.rsqrt(hid_sums[1] / FF - hid_mean * hid_mean + eps)
    hid_hat = (active - hid_mean[:, None]) * hid_inv[:, None]
    hid_low = rounded(hid_hat * hid_gain + hid_shift)
    result = lax.psum(jnp.dot(hid_low, down_weight, preferred_element_type=jnp.float32), "tensor")
    final = middle + result + down_bias
    output = rounded(final)
    upstream = cotangent.astype(jnp.float32)
    down_grad = jnp.einsum("tf,td->fd", hid_low, cotangent, preferred_element_type=jnp.float32)
    down_bias_grad = jnp.sum(upstream, 0)
    hid_back = jnp.einsum("td,fd->tf", cotangent, down_weight, preferred_element_type=jnp.float32)
    hid_gain_grad = jnp.sum(hid_back * hid_hat, 0)
    hid_shift_grad = jnp.sum(hid_back, 0)
    hid_scaled = hid_back * hid_gain
    hid_back_sums = lax.psum((jnp.sum(hid_scaled, 1), jnp.sum(hid_scaled * hid_hat, 1)), "tensor")
    active_grad = hid_inv[:, None] * (
        hid_scaled - hid_back_sums[0][:, None] / FF - hid_hat * hid_back_sums[1][:, None] / FF
    )
    slope = 0.5 * (1.0 + lax.erf(hidden * root_half)) + hidden * inv_root_two_pi * jnp.exp(
        -0.5 * hidden * hidden
    )
    hidden_grad = rounded(active_grad * slope)
    up_grad = jnp.einsum("td,tf->df", second, hidden_grad, preferred_element_type=jnp.float32)
    up_bias_grad = jnp.sum(hidden_grad, 0, dtype=jnp.float32)
    second_grad = lax.psum(
        jnp.einsum("tf,df->td", hidden_grad, up_weight, preferred_element_type=jnp.float32),
        "tensor",
    )
    ffn_gain_grad = jnp.sum(second_grad * ffn_hat, 0)
    ffn_shift_grad = jnp.sum(second_grad, 0)
    middle_grad = upstream + local_back(second_grad, ffn_hat, ffn_gain, ffn_inv)
    branch_low = rounded(middle_grad)
    out_bias_grad = jnp.sum(middle_grad, 0)
    out_grad = jnp.einsum("te,td->ed", mix_low, branch_low, preferred_element_type=jnp.float32)
    mix_back = jnp.einsum("td,ed->te", branch_low, out_weight, preferred_element_type=jnp.float32)
    mix_gain_grad = jnp.sum(mix_back * mix_hat, 0)
    mix_shift_grad = jnp.sum(mix_back, 0)
    mix_scaled = mix_back * mix_gain
    mix_back_sums = lax.psum((jnp.sum(mix_scaled, 1), jnp.sum(mix_scaled * mix_hat, 1)), "tensor")
    mixed_grad = mix_inv[:, None] * (
        mix_scaled - mix_back_sums[0][:, None] / D - mix_hat * mix_back_sums[1][:, None] / D
    )
    mixed_grad = rounded(mixed_grad).reshape(pairs, SLOT, local_heads, HD)
    again = jnp.exp(scores_of() - log_total)
    prob_grad = jnp.einsum("pqhd,pkhd->phqk", mixed_grad, value, preferred_element_type=jnp.float32)
    carried = jnp.sum(again * prob_grad, axis=-1, keepdims=True)
    score_grad = rounded(again * (prob_grad - carried))
    query_grad = (
        jnp.einsum("phqk,pkhd->pqhd", score_grad, key, preferred_element_type=jnp.float32) * scale
    )
    key_grad = (
        jnp.einsum("phqk,pqhd->pkhd", score_grad, query, preferred_element_type=jnp.float32) * scale
    )
    value_grad = jnp.einsum(
        "phqk,pqhd->pkhd", rounded(again), mixed_grad, preferred_element_type=jnp.float32
    )
    query_pre = rotate(query_grad, cosine, -sine, growth)
    key_pre = rotate(key_grad, cosine, -sine, shrink)
    proj_grad = rounded(jnp.stack([query_pre, key_pre, value_grad]).reshape(3, rows, local_width))
    qkv_grad = jnp.einsum("td,cte->cde", first, proj_grad, preferred_element_type=jnp.float32)
    qkv_bias_grad = jnp.sum(proj_grad, 1, dtype=jnp.float32)
    first_grad = lax.psum(
        jnp.einsum("cte,cde->td", proj_grad, qkv_weight, preferred_element_type=jnp.float32),
        "tensor",
    )
    pre_gain_grad = jnp.sum(first_grad * pre_hat, 0)
    pre_shift_grad = jnp.sum(first_grad, 0)
    tokens_grad = middle_grad + local_back(first_grad, pre_hat, pre_gain, pre_inv)
    qkv_part, out_part, up_part, down_part = (
        lax.psum_scatter(qkv_grad, "dp", scatter_dimension=1, tiled=True),
        lax.psum_scatter(out_grad, "dp", scatter_dimension=1, tiled=True),
        lax.psum_scatter(up_grad, "dp", scatter_dimension=0, tiled=True),
        lax.psum_scatter(down_grad, "dp", scatter_dimension=1, tiled=True),
    )
    small = lax.psum(
        (
            pre_gain_grad,
            pre_shift_grad,
            qkv_bias_grad,
            mix_gain_grad,
            mix_shift_grad,
            out_bias_grad,
            ffn_gain_grad,
            ffn_shift_grad,
            up_bias_grad,
            hid_gain_grad,
            hid_shift_grad,
            down_bias_grad,
        ),
        "dp",
    )
    return (
        output,
        tokens_grad,
        small[0],
        small[1],
        qkv_part,
        small[2],
        small[3],
        small[4],
        out_part,
        small[5],
        small[6],
        small[7],
        up_part,
        small[8],
        small[9],
        small[10],
        down_part,
        small[11],
    )


def solution(mesh):
    in_specs = (
        P("dp", None),
        P("dp"),
        P("dp", None),
        P(),
        P(),
        P(None, None, "tensor"),
        P(None, "tensor"),
        P("tensor"),
        P("tensor"),
        P("tensor", None),
        P(),
        P(),
        P(),
        P(None, "tensor"),
        P("tensor"),
        P("tensor"),
        P("tensor"),
        P("tensor", None),
        P(),
    )
    out_specs = (
        P("dp", None),
        P("dp", None),
        P(),
        P(),
        P(None, "dp", "tensor"),
        P(None, "tensor"),
        P("tensor"),
        P("tensor"),
        P("tensor", "dp"),
        P(),
        P(),
        P(),
        P("dp", "tensor"),
        P("tensor"),
        P("tensor"),
        P("tensor"),
        P("tensor", "dp"),
        P(),
    )
    return jax.shard_map(body, mesh=mesh, in_specs=in_specs, out_specs=out_specs, check_vma=False)
```

profile of v0, /device:TPU:0, one launch (start us, length us, event | category | flops | bytes accessed | tf_op | source)
XLA Modules:
  0.0 1522.1 jit_solution(11128239787350795962)
XLA Ops:
  10.9 11.5 add_bitcast_fusion
  60.9 4.8 reshape.334
  65.7 11.5 all-reduce.4
  77.3 7.4 fusion.52
  84.9 171.4 %all-reduce.11.cloned.1.call-done = f32[1024,2048]{1,0:T(8,128)} async-done(((f32[1024,2048]{1,0:T(8,128)}), f32[1024,2048]{1,0:T(8,128)}) %all-reduce.11.cloned.1.call-update) | async-done | bytes 8388624 | tf_op jit(solution)/shard_map/psum | solution.py:124
  256.3 5.6 fusion.58
  262.0 36.0 %fusion.57 = (f32[1024]{0:T(1024)S(1)}, f32[1024]{0:T(1024)S(1)}, f32[1024,2048]{1,0:T(8,128)}, f32[1024,2048]{1,0:T(8,128)}) fusion(f32[2048]{0:T(1024)S(1)} %copy-done.37, bf16[2048,2048]{1,0:T(8,128)(2,1)} %param.32, f32[1024,2048]{1,0:T(8,128)S(1)} %get-tuple-element.105, f32[2048]{0:T(1024)S(1)} %copy-done.44, f32[2048]{0:T(1024)S(1)} %copy-done.30, ...), kind=kOutput, calls=%fused_computation.139 | convolution fusion | flops 8743024640 | bytes 33595392 | tf_op jit(solution)/shard_map/dot_general | solution.py:128
  298.0 9.8 all-reduce.3
  307.8 17.3 %multiply_reduce_fusion = (f32[2048]{0:T(1024)}, f32[1024]{0:T(1024)S(1)}, f32[1024]{0:T(1024)S(1)}, f32[2048]{0:T(1024)}, f32[1024,2048]{1,0:T(8,128)}) fusion(f32[1024,2048]{1,0:T(8,128)} %get-tuple-element.104, f32[1024]{0:T(1024)S(1)} %get-tuple-element.126, f32[1024]{0:T(1024)S(1)} %get-tuple-element.125, f32[2048]{0:T(1024)S(1)} %copy-done.38, ...), kind=kOutput, calls=%fused_computation.29 | convolution fusion | flops 8608802816 | bytes 29401088 | tf_op jit(solution)/shard_map/td,fd->tf/dot_general | solution.py:141
  325.1 8.1 all-reduce.2
  333.2 12.3 convert_reduce_fusion.2
  347.5 13.2 fusion.68
  361.4 15.9 %fusion.56 = f32[1024,2048]{1,0:T(8,128)} fusion(bf16[2048,2048]{1,0:T(8,128)(2,1)} %param.36, f32[1024,2048]{1,0:T(8,128)} %get-tuple-element.104, f32[2048]{0:T(1024)S(1)} %copy-done.43, f32[2048]{0:T(1024)S(1)} %copy-done.38, f32[1024]{0:T(1024)S(1)} %get-tuple-element.126, f32[1024]{0:T(1024)S(1)} %get-tuple-element.125), kind=kOutput, calls=%fused_computation.138 | convolution fusion | flops 8600420352 | bytes 25190400 | tf_op jit(solution)/shard_map/dot_general | solution.py:135
  377.4 155.8 %all-reduce.13.cloned.1.call-done = f32[1024,2048]{1,0:T(8,128)} async-done(((f32[1024,2048]{1,0:T(8,128)}), f32[1024,2048]{1,0:T(8,128)}) %all-reduce.13.cloned.1.call-update) | async-done | bytes 8388624 | tf_op jit(solution)/shard_map/psum | solution.py:155
  533.1 8.3 multiply_reduce_fusion.1
  542.6 7.6 fusion.61
  554.8 9.8 all-reduce.1
  584.9 5.2 multiply_convert_fusion.5
  597.8 11.4 convolution_bitcast_fusion.1
  610.7 12.5 convolution_bitcast_fusion
  624.8 8.3 fusion.33
  635.9 280.1 %all-reduce.17.cloned.1.call-done = (f32[1024,2048]{1,0:T(8,128)}, f32[1024,2048]{1,0:T(8,128)}) async-done(((f32[1024,2048]{1,0:T(8,128)}, f32[1024,2048]{1,0:T(8,128)}), (f32[1024,2048]{1,0:T(8,128)}, f32[1024,2048]{1,0:T(8,128)})) %all-reduce.17.cloned.1.call-update) | async-done | bytes 16777232 | tf_op jit(solution)/shard_map/psum | solution.py:135
  916.0 7.1 fusion.18
  923.2 17.5 %fusion.55 = f32[2048,2048]{1,0:T(8,128)} fusion(bf16[1024,2048]{1,0:T(8,128)(2,1)} %param.21, f32[1024,2048]{1,0:T(8,128)} %get-tuple-element.104, f32[2048]{0:T(1024)S(1)} %copy-done.43, f32[2048]{0:T(1024)S(1)} %copy-done.38, f32[1024]{0:T(1024)S(1)} %get-tuple-element.126, f32[1024]{0:T(1024)S(1)} %get-tuple-element.125), kind=kOutput, calls=%fused_computation.137 | convolution fusion | flops 8600420352 | bytes 29384704 | tf_op jit(solution)/shard_map/tf,td->fd/dot_general | solution.py:139
  941.5 16.4 %fusion.53 = f32[2048,2048]{1,0:T(8,128)} fusion(bf16[1024,2048]{1,0:T(8,128)(2,1)} %copy-done.14, f32[1024,2048]{1,0:T(8,128)} %copy-done.2, f32[2048]{0:T(1024)S(1)} %copy-done.45, f32[2048]{0:T(1024)S(1)} %copy-done.30, f32[1024]{0:T(1024)S(1)} %get-tuple-element.128, f32[1024]{0:T(1024)S(1)} %get-tuple-element.127), kind=kOutput, calls=%fused_computation.135 | convolution fusion | flops 8600420352 | bytes 29384704 | tf_op jit(solution)/shard_map/td,tf->df/dot_general | solution.py:153
  958.6 10.4 add_convert_fusion
  969.0 9.7 fusion.17
  978.7 69.7 %reduce-scatter.5.cloned.1.call-done = f32[3,256,512]{1,2,0:T(8,128)} async-done(((f32[3,2048,512]{1,2,0:T(8,128)}), f32[3,256,512]{1,2,0:T(8,128)}) %reduce-scatter.5.cloned.1.call-update) | async-done | bytes 1572880 | tf_op jit(solution)/shard_map/reduce_scatter | solution.py:200
  1051.4 48.1 %reduce-scatter.7.cloned.1.call-done = f32[512,256]{1,0:T(8,128)} async-done(((f32[512,2048]{1,0:T(8,128)}), f32[512,256]{1,0:T(8,128)}) %reduce-scatter.7.cloned.1.call-update) | async-done | bytes 524304 | tf_op jit(solution)/shard_map/reduce_scatter | solution.py:201
  1099.5 56.9 %all-reduce.15.cloned.1.call-done = (f32[2048]{0:T(1024)}, f32[2048]{0:T(1024)}, f32[3,512]{1,0:T(4,128)}, f32[512]{0:T(512)}, f32[512]{0:T(512)}, /*index=5*/f3...) async-done(((f32[2048]{0:T(1024)}, f32[2048]{0:T(1024)}, f32[3,512]{1,0:T(4,128)}, ...) | async-done | bytes 83984 | tf_op jit(solution)/shard_map/psum | solution.py:205
  1156.4 173.4 %reduce-scatter.11.cloned.1.call-done = f32[2048,256]{1,0:T(8,128)} async-done(((f32[2048,2048]{1,0:T(8,128)}), f32[2048,256]{1,0:T(8,128)}) %reduce-scatter.11.cloned.1.call-update) | async-done | bytes 2097168 | tf_op jit(solution)/shard_map/reduce_scatter | solution.py:203
  1329.8 169.6 %reduce-scatter.9.cloned.1.call-done = f32[256,2048]{1,0:T(8,128)} async-done(((f32[2048,2048]{1,0:T(8,128)}), f32[256,2048]{1,0:T(8,128)}) %reduce-scatter.9.cloned.1.call-update) | async-done | bytes 2097168 | tf_op jit(solution)/shard_map/reduce_scatter | solution.py:202
  (185 shorter events, 104.1 us)
Async XLA Ops:
  7.2 70.1 %copy-start = (bf16[512,2048]{1,0:T(8,128)(2,1)S(1)}, bf16[512,2048]{1,0:T(8,128)(2,1)}, u32[]{:S(2)}) copy-start(bf16[512,2048]{1,0:T(8,128)(2,1)} %param.28) | copy-start | bytes 6291460
  7.2 249.1 %all-reduce.11.cloned.1.call-start = ((), (), s32[]{:S(2)}) async-start(), calls=%async_computation.4 | async-start | bytes 16777216 | tf_op jit(solution)/shard_map/psum | solution.py:124
  10.9 11.6 copy-start.26
  10.9 11.6 copy-start.28
  41.7 12.0 copy-start.8
  57.1 20.2 %copy-start.40 = (f32[512]{0:T(512)S(1)}, f32[512]{0:T(512)}, u32[]{:S(2)}) copy-start(f32[512]{0:T(512)} %param.26) | copy-start | bytes 6148
  57.1 20.2 %copy-start.46 = (f32[512]{0:T(512)S(1)}, f32[512]{0:T(512)}, u32[]{:S(2)}) copy-start(f32[512]{0:T(512)} %param.27) | copy-start | bytes 6148
  77.3 7.5 copy-start.32
  77.3 7.5 copy-start.34
  77.3 179.0 %copy-start.36 = (f32[2048]{0:T(1024)S(1)}, f32[2048]{0:T(1024)}, u32[]{:S(2)}) copy-start(f32[2048]{0:T(1024)} %param.29) | copy-start | bytes 24580
  84.8 177.2 %copy-start.30 = (f32[2048]{0:T(1024)S(1)}, f32[2048]{0:T(1024)}, u32[]{:S(2)}) copy-start(f32[2048]{0:T(1024)} %param.30) | copy-start | bytes 24580
  84.8 177.2 %copy-start.37 = (f32[2048]{0:T(1024)S(1)}, f32[2048]{0:T(1024)}, u32[]{:S(2)}) copy-start(f32[2048]{0:T(1024)} %param.33) | copy-start | bytes 24580
  84.8 177.2 %copy-start.44 = (f32[2048]{0:T(1024)S(1)}, f32[2048]{0:T(1024)}, u32[]{:S(2)}) copy-start(f32[2048]{0:T(1024)} %param.31) | copy-start | bytes 24580
  84.8 448.3 %all-reduce.13.cloned.1.call-start = ((), (), s32[]{:S(2)}) async-start(), calls=%async_computation.5 | async-start | bytes 16777216 | tf_op jit(solution)/shard_map/psum | solution.py:155
  261.9 36.0 %copy-start.2 = (f32[1024,2048]{1,0:T(8,128)}, f32[1024,2048]{1,0:T(8,128)S(1)}, u32[]{:S(2)}) copy-start(f32[1024,2048]{1,0:T(8,128)S(1)} %get-tuple-element.105) | copy-start | bytes 25165828
  262.0 45.8 %copy-start.38 = (f32[2048]{0:T(1024)S(1)}, f32[2048]{0:T(1024)}, u32[]{:S(2)}) copy-start(f32[2048]{0:T(1024)} %param.34) | copy-start | bytes 24580
  360.8 555.3 %all-reduce.17.cloned.1.call-start = ((), (), s32[]{:S(2)}) async-start(), calls=%async_computation.11 | async-start | bytes 33554432 | tf_op jit(solution)/shard_map/psum | solution.py:135
  533.1 8.4 copy-start.6
  533.1 9.4 copy-start.13
  542.5 7.6 copy-start.11
  542.5 7.6 copy-start.33
  542.5 7.6 copy-start.35
  542.5 7.6 copy-start.41
  577.4 7.4 copy-start.20
  584.8 10.5 copy-start.18
  609.2 439.2 %reduce-scatter.5.cloned.1.call-start = ((), (), s32[]{:S(2)}) async-start(), calls=%async_computation.6 | async-start | bytes 14155776 | tf_op jit(solution)/shard_map/reduce_scatter | solution.py:200
  623.2 476.3 %reduce-scatter.7.cloned.1.call-start = ((), (), s32[]{:S(2)}) async-start(), calls=%async_computation.7 | async-start | bytes 4718592 | tf_op jit(solution)/shard_map/reduce_scatter | solution.py:201
  633.1 523.3 %all-reduce.15.cloned.1.call-start = ((), (), s32[]{:S(2)}) async-start(), calls=%async_computation.10 | async-start | bytes 172032 | tf_op jit(solution)/shard_map/psum | solution.py:205
  923.2 406.6 %reduce-scatter.11.cloned.1.call-start = ((), (), s32[]{:S(2)}) async-start(), calls=%async_computation.9 | async-start | bytes 18874368 | tf_op jit(solution)/shard_map/reduce_scatter | solution.py:203
  940.8 558.6 %reduce-scatter.9.cloned.1.call-start = ((), (), s32[]{:S(2)}) async-start(), calls=%async_computation.8 | async-start | bytes 18874368 | tf_op jit(solution)/shard_map/reduce_scatter | solution.py:202
  958.6 10.4 copy-start.5
  969.0 545.8 %copy-start.1 = (bf16[512,2048]{1,0:T(8,128)(2,1)S(1)}, bf16[512,2048]{1,0:T(8,128)(2,1)}, u32[]{:S(2)}) copy-start(bf16[512,2048]{1,0:T(8,128)(2,1)} %param.28) | copy-start | bytes 6291460
  (25 other events, 86.6 us)
Sparse Core Ops, SparseCore 0:
  84.9 171.3 all-reduce.10
  360.9 172.1 all-reduce.12
  609.4 306.6 all-reduce.16
  918.2 130.1 reduce-scatter.4
  1051.1 48.3 reduce-scatter.6
  1104.5 51.8 all-reduce.14
  1159.3 170.4 reduce-scatter.10
  1332.8 166.6 reduce-scatter.8
where the time goes:
time: 1530 us; the launch traced here: 1520 us
  waiting for transfers between devices  1130 us (74%)
  matrix products  185 us (12%)
  other arithmetic  82.8 us (5%)
  local copies, waits for them, and re-layouts  73.6 us (5%)
  blocking collectives  39.2 us (3%)
  between operations  15.4 us (1%)
    psum x1, waiting for transfers between devices, body(): lax.psum(jnp.dot(hid_low, down_weight, preferred_element_type=jnp.float32...  280 us
    reduce_scatter x1, waiting for transfers between devices, body(): lax.psum_scatter(down_grad, 'dp', scatter_dimension=1, tiled=True)  173 us
    psum x1, waiting for transfers between devices, body(): lax.psum(jnp.dot(mix_low, out_weight, preferred_element_type=jnp.float32)...  171 us
    reduce_scatter x1, waiting for transfers between devices, body(): lax.psum_scatter(up_grad, 'dp', scatter_dimension=0, tiled=True)  170 us
    psum x1, waiting for transfers between devices, body(): lax.psum(jnp.einsum('tf,df->td', hidden_grad, up_weight, preferred_elemen...  156 us
    reduce_scatter x1, waiting for transfers between devices, body(): lax.psum_scatter(qkv_grad, 'dp', scatter_dimension=1, tiled=True)  69.7 us
    psum x1, waiting for transfers between devices, body(): lax.psum((pre_gain_grad, pre_shift_grad, qkv_bias_grad, mix_gain_grad, mi...  56.9 us
    reduce_scatter x1, waiting for transfers between devices, body(): lax.psum_scatter(out_grad, 'dp', scatter_dimension=1, tiled=True)  48.1 us
  transfers between devices with their start and end apart: 8, of which 8 were waited for; matrix products, arithmetic and copies ran while one was open for 7% of the time, Pallas kernels for 0%

commit v1 on v0

--- a/solution.py
+++ b/solution.py
@@ -132,7 +132,9 @@
     hid_inv = lax.rsqrt(hid_sums[1] / FF - hid_mean * hid_mean + eps)
     hid_hat = (active - hid_mean[:, None]) * hid_inv[:, None]
     hid_low = rounded(hid_hat * hid_gain + hid_shift)
-    result = lax.psum(jnp.dot(hid_low, down_weight, preferred_element_type=jnp.float32), "tensor")
+    s0 = jnp.dot(hid_low, down_weight, preferred_element_type=jnp.float32)
+    taken_in = lax.all_gather(s0, axis_name="tensor")
+    result = jnp.sum(taken_in, axis=0)
     final = middle + result + down_bias
     output = rounded(final)
     upstream = cotangent.astype(jnp.float32)

time: 1530 us -> 1720 us (1.12)
  waiting for transfers between devices: 1130 us -> 1290 us
  other arithmetic: 82.8 us -> 101 us
    all_gather x0 -> x1, waiting for transfers between devices: none -> 291 us  [body(): taken_in = lax.all_gather(s0, axis_name='tensor')]
    psum x1, waiting for transfers between devices: 280 us -> 112 us  [body(): lax.psum(jnp.einsum('cte,cde->td', proj_grad, qkv_weight, preferred_eleme...]
    reduce_scatter x1, waiting for transfers between devices: 69.7 us -> 112 us  [body(): lax.psum_scatter(qkv_grad, 'dp', scatter_dimension=1, tiled=True)]
  transfers between devices with their start and end apart: 8 -> 9, of which waited for: 8 -> 9; matrix products, arithmetic and copies ran while one was open for 7% -> 6% of each run, Pallas kernels for 0% -> 0%
where the time goes in v1:
time: 1720 us; the launch traced here: 1710 us
  waiting for transfers between devices  1290 us (75%)
  matrix products  185 us (11%)
  other arithmetic  101 us (6%)
  local copies, waits for them, and re-layouts  82.2 us (5%)
  blocking collectives  38.4 us (2%)
    all_gather x1, waiting for transfers between devices, body(): taken_in = lax.all_gather(s0, axis_name='tensor')  291 us
    psum x1, waiting for transfers between devices, body(): lax.psum(jnp.dot(mix_low, out_weight, preferred_element_type=jnp.float32)...  171 us
    reduce_scatter x1, waiting for transfers between devices, body(): lax.psum_scatter(up_grad, 'dp', scatter_dimension=0, tiled=True)  170 us
    reduce_scatter x1, waiting for transfers between devices, body(): lax.psum_scatter(down_grad, 'dp', scatter_dimension=1, tiled=True)  166 us
    psum x1, waiting for transfers between devices, body(): lax.psum(jnp.einsum('tf,df->td', hidden_grad, up_weight, preferred_elemen...  155 us
    psum x1, waiting for transfers between devices, body(): lax.psum(jnp.einsum('cte,cde->td', proj_grad, qkv_weight, preferred_eleme...  112 us
    reduce_scatter x1, waiting for transfers between devices, body(): lax.psum_scatter(qkv_grad, 'dp', scatter_dimension=1, tiled=True)  112 us
    psum x1, waiting for transfers between devices, body(): lax.psum((pre_gain_grad, pre_shift_grad, qkv_bias_grad, mix_gain_grad, mi...  57 us
  transfers between devices with their start and end apart: 9, of which 9 were waited for; matrix products, arithmetic and copies ran while one was open for 6% of the time, Pallas kernels for 0%

profile of v1, /device:TPU:0, one launch (start us, length us, event | category | flops | bytes accessed | tf_op | source)
XLA Modules:
  0.0 1708.8 jit_solution(16560110769707821327)
XLA Ops:
  10.9 11.5 add_bitcast_fusion
  65.8 11.5 all-reduce.4
  77.9 7.4 fusion.52
  85.4 171.5 %all-reduce.10.cloned.1.call-done = f32[1024,2048]{1,0:T(8,128)} async-done(((f32[1024,2048]{1,0:T(8,128)}), f32[1024,2048]{1,0:T(8,128)}) %all-reduce.10.cloned.1.call-update) | async-done | bytes 8388624 | tf_op jit(solution)/shard_map/psum | solution.py:124
  256.9 5.6 fusion.58
  262.6 36.0 %fusion.57 = (f32[1024]{0:T(1024)S(1)}, f32[1024]{0:T(1024)S(1)}, f32[1024,2048]{1,0:T(8,128)}, f32[1024,2048]{1,0:T(8,128)}) fusion(f32[2048]{0:T(1024)S(1)} %copy-done.34, bf16[2048,2048]{1,0:T(8,128)(2,1)} %param.32, f32[1024,2048]{1,0:T(8,128)S(1)} %get-tuple-element.103, f32[2048]{0:T(1024)S(1)} %copy-done.41, f32[2048]{0:T(1024)S(1)} %copy-done.27, ...), kind=kOutput, calls=%fused_computation.139 | convolution fusion | flops 8743024640 | bytes 33595392 | tf_op jit(solution)/shard_map/dot_general | solution.py:128
  298.6 9.8 all-reduce.3
  308.4 17.3 %multiply_reduce_fusion = (f32[2048]{0:T(1024)}, f32[1024]{0:T(1024)S(1)}, f32[1024]{0:T(1024)S(1)}, f32[2048]{0:T(1024)}, f32[1024,2048]{1,0:T(8,128)}) fusion(f32[1024,2048]{1,0:T(8,128)} %get-tuple-element.102, f32[1024]{0:T(1024)S(1)} %get-tuple-element.125, f32[1024]{0:T(1024)S(1)} %get-tuple-element.124, f32[2048]{0:T(1024)S(1)} %copy-done.35, ...), kind=kOutput, calls=%fused_computation.29 | convolution fusion | flops 8608802816 | bytes 29401088 | tf_op jit(solution)/shard_map/td,fd->tf/dot_general | solution.py:143
  325.7 8.1 all-reduce.2
  333.8 12.2 convert_reduce_fusion.2
  348.0 13.2 fusion.68
  361.9 16.0 fusion.56
  378.7 154.9 %all-reduce.12.cloned.1.call-done = f32[1024,2048]{1,0:T(8,128)} async-done(((f32[1024,2048]{1,0:T(8,128)}), f32[1024,2048]{1,0:T(8,128)}) %all-reduce.12.cloned.1.call-update) | async-done | bytes 8388624 | tf_op jit(solution)/shard_map/psum | solution.py:157
  533.6 8.2 multiply_reduce_fusion.1
  541.8 291.4 %all-gather.3.cloned.1.call-done = f32[4096,2048]{1,0:T(8,128)} async-done(((f32[1024,2048]{1,0:T(8,128)}), f32[4096,2048]{1,0:T(8,128)}) %all-gather.3.cloned.1.call-update) | async-done | bytes 33554448 | tf_op jit(solution)/shard_map/all_gather | solution.py:136
  833.3 15.9 reduce_sum.294
  849.2 15.0 fusion.61
  868.9 9.1 all-reduce.1
  900.3 5.3 multiply_convert_fusion.5
  923.4 11.4 convolution_bitcast_fusion.1
  935.5 12.8 convolution_bitcast_fusion
  948.4 16.6 fusion.55
  965.7 16.7 fusion.53
  983.1 8.6 fusion.33
  994.6 112.4 %all-reduce.14.cloned.1.call-done = f32[1024,2048]{1,0:T(8,128)} async-done(((f32[1024,2048]{1,0:T(8,128)}), f32[1024,2048]{1,0:T(8,128)}) %all-reduce.14.cloned.1.call-update) | async-done | bytes 8388624 | tf_op jit(solution)/shard_map/psum | solution.py:194
  1107.0 7.1 fusion.18
  1114.2 13.0 fusion.17
  1127.2 111.8 %reduce-scatter.5.cloned.1.call-done = f32[3,256,512]{1,2,0:T(8,128)} async-done(((f32[3,2048,512]{1,2,0:T(8,128)}), f32[3,256,512]{1,2,0:T(8,128)}) %reduce-scatter.5.cloned.1.call-update) | async-done | bytes 1572880 | tf_op jit(solution)/shard_map/reduce_scatter | solution.py:202
  1242.1 166.4 %reduce-scatter.11.cloned.1.call-done = f32[2048,256]{1,0:T(8,128)} async-done(((f32[2048,2048]{1,0:T(8,128)}), f32[2048,256]{1,0:T(8,128)}) %reduce-scatter.11.cloned.1.call-update) | async-done | bytes 2097168 | tf_op jit(solution)/shard_map/reduce_scatter | solution.py:205
  1408.5 169.6 %reduce-scatter.9.cloned.1.call-done = f32[256,2048]{1,0:T(8,128)} async-done(((f32[2048,2048]{1,0:T(8,128)}), f32[256,2048]{1,0:T(8,128)}) %reduce-scatter.9.cloned.1.call-update) | async-done | bytes 2097168 | tf_op jit(solution)/shard_map/reduce_scatter | solution.py:204
  1578.0 51.3 %reduce-scatter.7.cloned.1.call-done = f32[512,256]{1,0:T(8,128)} async-done(((f32[512,2048]{1,0:T(8,128)}), f32[512,256]{1,0:T(8,128)}) %reduce-scatter.7.cloned.1.call-update) | async-done | bytes 524304 | tf_op jit(solution)/shard_map/reduce_scatter | solution.py:203
  1629.3 57.0 %all-reduce.16.cloned.1.call-done = (f32[2048]{0:T(1024)}, f32[2048]{0:T(1024)}, f32[3,512]{1,0:T(4,128)}, f32[512]{0:T(512)}, f32[512]{0:T(512)}, /*index=5*/f3...) async-done(((f32[2048]{0:T(1024)}, f32[2048]{0:T(1024)}, f32[3,512]{1,0:T(4,128)}, ...) | async-done | bytes 83984 | tf_op jit(solution)/shard_map/psum | solution.py:207
  (182 shorter events, 119.1 us)
Async XLA Ops:
  7.2 70.7 %copy-start = (bf16[512,2048]{1,0:T(8,128)(2,1)S(1)}, bf16[512,2048]{1,0:T(8,128)(2,1)}, u32[]{:S(2)}) copy-start(bf16[512,2048]{1,0:T(8,128)(2,1)} %param.28) | copy-start | bytes 6291460
  7.2 249.7 %all-reduce.10.cloned.1.call-start = ((), (), s32[]{:S(2)}) async-start(), calls=%async_computation.4 | async-start | bytes 16777216 | tf_op jit(solution)/shard_map/psum | solution.py:124
  10.9 11.6 copy-start.23
  10.9 11.6 copy-start.25
  37.2 6.8 copy-start.45
  41.7 12.0 copy-start.5
  57.1 20.8 %copy-start.37 = (f32[512]{0:T(512)S(1)}, f32[512]{0:T(512)}, u32[]{:S(2)}) copy-start(f32[512]{0:T(512)} %param.26) | copy-start | bytes 6148
  57.1 20.8 %copy-start.43 = (f32[512]{0:T(512)S(1)}, f32[512]{0:T(512)}, u32[]{:S(2)}) copy-start(f32[512]{0:T(512)} %param.27) | copy-start | bytes 6148
  77.9 179.0 %copy-start.33 = (f32[2048]{0:T(1024)S(1)}, f32[2048]{0:T(1024)}, u32[]{:S(2)}) copy-start(f32[2048]{0:T(1024)} %param.29) | copy-start | bytes 24580
  85.3 177.2 %copy-start.27 = (f32[2048]{0:T(1024)S(1)}, f32[2048]{0:T(1024)}, u32[]{:S(2)}) copy-start(f32[2048]{0:T(1024)} %param.30) | copy-start | bytes 24580
  85.4 177.2 %copy-start.34 = (f32[2048]{0:T(1024)S(1)}, f32[2048]{0:T(1024)}, u32[]{:S(2)}) copy-start(f32[2048]{0:T(1024)} %param.33) | copy-start | bytes 24580
  85.4 177.2 %copy-start.41 = (f32[2048]{0:T(1024)S(1)}, f32[2048]{0:T(1024)}, u32[]{:S(2)}) copy-start(f32[2048]{0:T(1024)} %param.31) | copy-start | bytes 24580
  85.4 448.2 %all-reduce.12.cloned.1.call-start = ((), (), s32[]{:S(2)}) async-start(), calls=%async_computation.5 | async-start | bytes 16777216 | tf_op jit(solution)/shard_map/psum | solution.py:157
  262.5 36.1 %copy-start.3 = (f32[1024,2048]{1,0:T(8,128)}, f32[1024,2048]{1,0:T(8,128)S(1)}, u32[]{:S(2)}) copy-start(f32[1024,2048]{1,0:T(8,128)S(1)} %get-tuple-element.103) | copy-start | bytes 25165828
  262.6 45.8 %copy-start.35 = (f32[2048]{0:T(1024)S(1)}, f32[2048]{0:T(1024)}, u32[]{:S(2)}) copy-start(f32[2048]{0:T(1024)} %param.34) | copy-start | bytes 24580
  361.2 472.0 %all-gather.3.cloned.1.call-start = ((), (), s32[]{:S(2)}) async-start(), calls=%async_computation.11 | async-start | bytes 41943040 | tf_op jit(solution)/shard_map/all_gather | solution.py:136
  378.0 729.1 %all-reduce.14.cloned.1.call-start = ((), (), s32[]{:S(2)}) async-start(), calls=%async_computation.6 | async-start | bytes 16777216 | tf_op jit(solution)/shard_map/psum | solution.py:194
  833.3 15.9 copy-start.36
  849.2 15.0 copy-start.8
  849.2 15.0 copy-start.30
  849.2 15.0 copy-start.32
  849.2 15.0 copy-start.38
  892.9 7.4 copy-start.15
  892.9 7.4 copy-start.17
  892.9 7.4 copy-start.19
  892.9 7.4 copy-start.22
  900.3 17.9 %copy-start.11 = (bf16[8,128,8,64]{1,3,2,0:T(8,128)(2,1)S(1)}, bf16[8,128,8,64]{1,3,2,0:T(8,128)(2,1)}, u32[]{:S(2)}) copy-start(bf16[8,128,8,64]{1,3,2,0:T(8,128)(2,1)} %fusion.43) | copy-start | bytes 3145732
  934.9 304.2 %reduce-scatter.5.cloned.1.call-start = ((), (), s32[]{:S(2)}) async-start(), calls=%async_computation.7 | async-start | bytes 14155776 | tf_op jit(solution)/shard_map/reduce_scatter | solution.py:202
  948.3 460.1 %reduce-scatter.11.cloned.1.call-start = ((), (), s32[]{:S(2)}) async-start(), calls=%async_computation.10 | async-start | bytes 18874368 | tf_op jit(solution)/shard_map/reduce_scatter | solution.py:205
  965.0 613.0 %reduce-scatter.9.cloned.1.call-start = ((), (), s32[]{:S(2)}) async-start(), calls=%async_computation.9 | async-start | bytes 18874368 | tf_op jit(solution)/shard_map/reduce_scatter | solution.py:204
  982.4 646.9 %reduce-scatter.7.cloned.1.call-start = ((), (), s32[]{:S(2)}) async-start(), calls=%async_computation.8 | async-start | bytes 4718592 | tf_op jit(solution)/shard_map/reduce_scatter | solution.py:203
  991.7 694.6 %all-reduce.16.cloned.1.call-start = ((), (), s32[]{:S(2)}) async-start(), calls=%async_computation.12 | async-start | bytes 172032 | tf_op jit(solution)/shard_map/psum | solution.py:207
  (23 other events, 56.7 us)
Sparse Core Ops, SparseCore 0:
  85.5 171.3 all-reduce.9
  361.4 172.2 all-reduce.11
  535.5 297.7 all-gather.2
  935.0 172.0 all-reduce.13
  1109.2 129.8 reduce-scatter.4
  1241.8 166.6 reduce-scatter.10
  1411.4 166.5 reduce-scatter.8
  1580.9 48.3 reduce-scatter.6
  1634.5 51.8 all-reduce.15
